TPU v7x, 32 devices: a whole 2x2x4 slice. The times are simulated.
32 devices in a mesh: dp: 8 (over y, x, core), tensor: 4 (over z).
Axes of the slice: x: 2, y: 2, z: 4, core: 2. Of those that a mesh axis runs over, the one named last changes fastest.
Arguments:
- tokens: bfloat16 [32, 1024, 512], P(('dp', 'tensor')), may hold values from -6 to 6
- timestep: int32 [32], P(('dp', 'tensor')), may hold values from 0 to 999
- segment_ids: int32 [32, 1024], P('dp'), may hold values from 0 to 7, never falling along the last dimension, each value on 1 to 512 neighbouring positions
- span_lengths: int32 [32], P('dp'), may hold values from 512 to 1024
- w_qkv: float32 [3, 512, 512], P(None, 'dp', 'tensor'), may hold values from -0.25 to 0.25
- w_out_t: float32 [512, 512], P('dp', 'tensor'), may hold values from -1.5 to 1.5
- w_up: float32 [512, 2048], P('dp', 'tensor'), may hold values from -0.25 to 0.25
- w_down_t: float32 [512, 2048], P('dp', 'tensor'), may hold values from -0.125 to 0.125
- w_time: float32 [512, 512], replicated, may hold values from -0.25 to 0.25
- b_time: float32 [512], replicated, may hold values from -3 to 3
- ln1_gain: float32 [512], replicated, may hold values from 0.1 to 1.9
- ln1_bias: float32 [512], replicated, may hold values from -3 to 3
- ln2_gain: float32 [512], replicated, may hold values from 0.1 to 1.9
- ln2_bias: float32 [512], replicated, may hold values from -3 to 3
- b_up: float32 [2048], replicated, may hold values from -3 to 3
- b_down: float32 [512], replicated, may hold values from -3 to 3
- cotangent: bfloat16 [32, 1024, 512], P(('dp', 'tensor')), may hold values from -6 to 6
Outputs:
- layer_out: bfloat16 [32, 1024, 512], P(('dp', 'tensor'))
- grad_tokens: float32 [32, 1024, 512], P(('dp', 'tensor'))
- grad_w_qkv: float32 [3, 512, 512], P(None, 'dp', 'tensor')
- grad_w_out_t: float32 [512, 512], P('dp', 'tensor')
- grad_w_up: float32 [512, 2048], P('dp', 'tensor')
- grad_w_down_t: float32 [512, 2048], P('dp', 'tensor')
- grad_w_time: float32 [512, 512], replicated
- grad_b_time: float32 [512], replicated
- grad_ln1_gain: float32 [512], replicated
- grad_ln1_bias: float32 [512], replicated
- grad_ln2_gain: float32 [512], replicated
- grad_ln2_bias: float32 [512], replicated
- grad_b_up: float32 [2048], replicated
- grad_b_down: float32 [512], replicated
Inputs may be any that keep to these rules, and one draw needn't show every extreme that they name: `segment_ids`: never falls along a row; each document has 1 to 512 positions and one has exactly that many.
All inputs are finite; a program needn't handle non-finite values.
Results may differ from a plain program's by a relative error of at most 0.013.
Values may be sent and summed in bfloat16 or wider, within the bound.
A program may use at most 192 MiB of HBM per device.

v0:
```python
import math
import jax
import jax.numpy as jnp
from jax import lax
from jax.sharding import PartitionSpec as P

HS = 64
FF = 2048
highest = lax.Precision.HIGHEST
epsilon = 1e-05
masked_score = -1e30


def split_up(value, dim, count):
    before, after = (value.shape[:dim], value.shape[dim + 1 :])
    return jnp.moveaxis(value.reshape(*before, count, -1, *after), dim, 0)


def sent_and_summed(value, axis, dim):
    count = lax.axis_size(axis)
    parts = lax.all_to_all(split_up(value, dim, count), axis, 0, 0, tiled=True)
    return jnp.sum(parts.astype(jnp.float32), axis=0)


def side_by_side(arrays, axis, dim, along):
    ends, at = ([], 0)
    for a in arrays[:-1]:
        at += a.shape[along]
        ends.append(at)
    both = jnp.concatenate(arrays, axis=along)
    return tuple(jnp.split(sent_and_summed(both, axis, dim), ends, axis=along))


def norm_layer(values, gain_vec, shift_vec):
    row_mean = jnp.mean(values, axis=-1, keepdims=True)
    centred = values - row_mean
    variance = jnp.mean(centred * centred, axis=-1, keepdims=True)
    return centred * lax.rsqrt(variance + epsilon) * gain_vec + shift_vec


def time_features(timestep, features):
    half_width = features // 2
    frequency = jnp.exp(-math.log(10000.0) * jnp.arange(half_width, dtype=jnp.float32) / half_width)
    angles = timestep.astype(jnp.float32)[:, None] * frequency[None, :]
    return jnp.concatenate([jnp.sin(angles), jnp.cos(angles)], axis=1)


def allowed_keys(segment, length):
    places = jnp.arange(segment.shape[0], dtype=jnp.int32)
    same_doc = segment[:, None] == segment[None, :]
    is_valid = (places < length)[None, :] | (places[:, None] == places[None, :])
    return same_doc & is_valid


def gelu_tanh(values):
    return jax.nn.gelu(values, approximate=True)


def split_heads(values):
    return values.reshape(values.shape[0], values.shape[1] // HS, HS)


def head_scores(query_heads, key_heads, allowed):
    scores = jnp.einsum(
        "qhe,khe->hqk", query_heads, key_heads, preferred_element_type=jnp.float32
    ) * (1.0 / math.sqrt(HS))
    return jnp.where(allowed[None], scores, masked_score)


def attend_forward(packed):
    query_heads = split_heads(packed[0])
    key_heads = split_heads(packed[1])
    value_heads = split_heads(packed[2])
    scores = head_scores(query_heads, key_heads, allowed_keys(packed[3], packed[4]))
    row_max = jnp.max(scores, axis=-1, keepdims=True)
    raised = jnp.exp(scores - row_max)
    row_total = jnp.sum(raised, axis=-1, keepdims=True)
    probs_low = (raised / row_total).astype(jnp.bfloat16)
    mixed = jnp.einsum("hqk,khe->qhe", probs_low, value_heads, preferred_element_type=jnp.float32)
    return (mixed.reshape(packed[0].shape).astype(jnp.bfloat16), row_max + jnp.log(row_total))


def attend_backward(packed):
    query_heads = split_heads(packed[0])
    key_heads = split_heads(packed[1])
    value_heads = split_heads(packed[2])
    grad_heads = split_heads(packed[3])
    scores = head_scores(query_heads, key_heads, allowed_keys(packed[5], packed[6]))
    attn_probs = jnp.exp(scores - packed[4])
    probs_low = attn_probs.astype(jnp.bfloat16)
    grad_values = jnp.einsum(
        "hqk,qhe->khe", probs_low, grad_heads, preferred_element_type=jnp.float32
    )
    grad_probs = jnp.einsum(
        "qhe,khe->hqk", grad_heads, value_heads, preferred_element_type=jnp.float32
    )
    row_delta = jnp.sum(attn_probs * grad_probs, axis=-1, keepdims=True)
    grad_scores = (attn_probs * (grad_probs - row_delta)).astype(jnp.bfloat16)
    score_scale = 1.0 / math.sqrt(HS)
    grad_queries = (
        jnp.einsum("hqk,khe->qhe", grad_scores, key_heads, preferred_element_type=jnp.float32)
        * score_scale
    )
    grad_keys = (
        jnp.einsum("hqk,qhe->khe", grad_scores, query_heads, preferred_element_type=jnp.float32)
        * score_scale
    )
    shape_rows = packed[0].shape
    return jnp.stack(
        [
            grad_queries.reshape(shape_rows),
            grad_keys.reshape(shape_rows),
            grad_values.reshape(shape_rows),
        ]
    ).astype(jnp.bfloat16)


def shards(
    tokens,
    timestep,
    segment_ids,
    span_lengths,
    w_qkv,
    w_out_t,
    w_up,
    w_down_t,
    w_time,
    b_time,
    ln1_gain,
    ln1_bias,
    ln2_gain,
    ln2_bias,
    b_up,
    b_down,
    cotangent,
):
    tensor_place = lax.axis_index("tensor")
    qkv_copy, out_copy, up_copy, down_copy = (
        lax.all_gather(w_qkv.astype(jnp.bfloat16), "dp", axis=1, tiled=True),
        lax.all_gather(w_out_t.astype(jnp.bfloat16), "dp", axis=0, tiled=True),
        lax.all_gather(w_up.astype(jnp.bfloat16), "dp", axis=0, tiled=True),
        lax.all_gather(w_down_t.astype(jnp.bfloat16), "dp", axis=0, tiled=True),
    )
    bias_up_cols = lax.dynamic_slice_in_dim(
        b_up, tensor_place * up_copy.shape[1], up_copy.shape[1], 0
    )
    ff_cols = up_copy.shape[1]
    time_emb = time_features(timestep, tokens.shape[2])
    time_proj = jnp.dot(time_emb, w_time, precision=highest) + b_time
    start = tokens.astype(jnp.float32) + time_proj[:, None, :]
    normed_one = norm_layer(start, ln1_gain, ln1_bias).astype(jnp.bfloat16)
    normed_all = lax.all_gather(normed_one, "tensor", axis=0, tiled=True)
    qkv_act = jnp.einsum(
        "nsd,cde->cnse", normed_all, qkv_copy, preferred_element_type=jnp.float32
    ).astype(jnp.bfloat16)
    mixed, log_total = lax.map(
        attend_forward, (qkv_act[0], qkv_act[1], qkv_act[2], segment_ids, span_lengths)
    )
    part_rows = mixed
    attn_out = lax.psum_scatter(
        jnp.einsum("nse,de->nsd", part_rows, out_copy, preferred_element_type=jnp.float32),
        "tensor",
        scatter_dimension=0,
        tiled=True,
    )
    middle = start + attn_out
    normed_two = norm_layer(middle, ln2_gain, ln2_bias).astype(jnp.bfloat16)
    second_all = lax.all_gather(normed_two, "tensor", axis=0, tiled=True)
    upper = (
        jnp.einsum("nsd,df->nsf", second_all, up_copy, preferred_element_type=jnp.float32)
        + bias_up_cols
    )
    activated = gelu_tanh(upper).astype(jnp.bfloat16)
    part_rows = activated
    ffn_out = lax.psum_scatter(
        jnp.einsum("nsf,df->nsd", part_rows, down_copy, preferred_element_type=jnp.float32).astype(
            jnp.bfloat16
        ),
        "tensor",
        scatter_dimension=0,
        tiled=True,
    ).astype(jnp.float32)
    layer_out = (middle + ffn_out + b_down).astype(jnp.bfloat16)
    grad_b_down = jnp.sum(cotangent.astype(jnp.float32), axis=(0, 1))
    grad_out_all = lax.all_gather(cotangent, "tensor", axis=0, tiled=True)
    grad_down = jnp.einsum(
        "nsd,nsf->df", grad_out_all, activated, preferred_element_type=jnp.float32
    )
    grad_act = jnp.einsum(
        "nsd,df->nsf", grad_out_all, down_copy, preferred_element_type=jnp.float32
    )
    gelu_value, gelu_pull = jax.vjp(gelu_tanh, upper)
    grad_upper = gelu_pull(grad_act)[0].astype(jnp.bfloat16)
    grad_bias_cols = jnp.sum(grad_upper.astype(jnp.float32), axis=(0, 1))
    grad_up = jnp.einsum("nsd,nsf->df", second_all, grad_upper, preferred_element_type=jnp.float32)
    part_rows = grad_upper
    grad_normed_two = lax.psum_scatter(
        jnp.einsum("nsf,df->nsd", part_rows, up_copy, preferred_element_type=jnp.float32).astype(
            jnp.bfloat16
        ),
        "tensor",
        scatter_dimension=0,
        tiled=True,
    ).astype(jnp.float32)
    norm_two_value, norm_two_pull = jax.vjp(norm_layer, middle, ln2_gain, ln2_bias)
    grad_middle_norm, grad_gain_two, grad_bias_two = norm_two_pull(grad_normed_two)
    grad_middle = cotangent.astype(jnp.float32) + grad_middle_norm
    grad_attn = grad_middle.astype(jnp.bfloat16)
    grad_attn_all = lax.all_gather(grad_attn, "tensor", axis=0, tiled=True)
    grad_out_w = jnp.einsum("nsd,nse->de", grad_attn_all, mixed, preferred_element_type=jnp.float32)
    grad_mixed = jnp.einsum(
        "nsd,de->nse", grad_attn_all, out_copy, preferred_element_type=jnp.float32
    ).astype(jnp.bfloat16)
    grad_qkv_act = lax.map(
        attend_backward,
        (qkv_act[0], qkv_act[1], qkv_act[2], grad_mixed, log_total, segment_ids, span_lengths),
    )
    grad_qkv_w = jnp.einsum(
        "nsd,ncse->cde", normed_all, grad_qkv_act, preferred_element_type=jnp.float32
    )
    part_rows = grad_qkv_act
    grad_normed_one = lax.psum_scatter(
        jnp.einsum("ncse,cde->nsd", part_rows, qkv_copy, preferred_element_type=jnp.float32).astype(
            jnp.bfloat16
        ),
        "tensor",
        scatter_dimension=0,
        tiled=True,
    ).astype(jnp.float32)
    norm_one_value, norm_one_pull = jax.vjp(norm_layer, start, ln1_gain, ln1_bias)
    grad_start_norm, grad_gain_one, grad_bias_one = norm_one_pull(grad_normed_one)
    grad_tokens = grad_middle + grad_start_norm
    grad_time_rows = jnp.sum(grad_tokens, axis=1)
    grad_time_w = jnp.dot(time_emb.T, grad_time_rows, precision=highest)
    grad_time_bias = jnp.sum(grad_time_rows, axis=0)
    grad_bias_up = lax.dynamic_update_slice_in_dim(
        jnp.zeros((FF,), jnp.float32), grad_bias_cols, tensor_place * ff_cols, 0
    )
    shard_qkv, shard_out, shard_up, shard_down = (
        sent_and_summed(grad_qkv_w.astype(jnp.bfloat16), "dp", 1),
        *side_by_side(
            (
                grad_out_w.astype(jnp.bfloat16),
                grad_up.astype(jnp.bfloat16),
                grad_down.astype(jnp.bfloat16),
            ),
            "dp",
            0,
            1,
        ),
    )
    summed = lax.psum(
        (
            grad_time_w,
            grad_time_bias,
            grad_gain_one,
            grad_bias_one,
            grad_gain_two,
            grad_bias_two,
            grad_bias_up,
            grad_b_down,
        ),
        ("dp", "tensor"),
    )
    return (
        layer_out,
        grad_tokens,
        shard_qkv,
        shard_out,
        shard_up,
        shard_down,
        summed[0],
        summed[1],
        summed[2],
        summed[3],
        summed[4],
        summed[5],
        summed[6],
        summed[7],
    )


def solution(mesh):
    return jax.shard_map(
        shards,
        mesh=mesh,
        in_specs=(
            P(("dp", "tensor"), None, None),
            P(("dp", "tensor")),
            P("dp", None),
            P("dp"),
            P(None, "dp", "tensor"),
            P("dp", "tensor"),
            P("dp", "tensor"),
            P("dp", "tensor"),
            P(),
            P(),
            P(),
            P(),
            P(),
            P(),
            P(),
            P(),
            P(("dp", "tensor"), None, None),
        ),
        out_specs=(
            P(("dp", "tensor"), None, None),
            P(("dp", "tensor"), None, None),
            P(None, "dp", "tensor"),
            P("dp", "tensor"),
            P("dp", "tensor"),
            P("dp", "tensor"),
            P(),
            P(),
            P(),
            P(),
            P(),
            P(),
            P(),
            P(),
        ),
        check_vma=False,
    )
```

profile of v0, /device:TPU:0, one launch (start us, length us, event | category | flops | bytes accessed | tf_op | source)
XLA Modules:
  0.0 1040.7 jit_solution(14734776910179383602)
XLA Ops:
  15.9 10.7 %all_gather.26 = bf16[512,128]{1,0:T(8,128)(2,1)S(1)} all-gather(bf16[64,128]{1,0:T(8,128)(2,1)S(1)} %convert_element_type.133), channel_id=1, replica_groups=mesh['dp'=8,'tensor'=4] {'dp'}, dimensions={0}, use_global_device_ids=true | all-gather | bytes 147456 | tf_op jit(solution)/shard_map/all_gather | solution.py:140
  26.6 9.7 all_gather.25
  36.3 63.1 %all-gather.5.cloned.1.call-done = bf16[4,1024,512]{2,1,0:T(8,128)(2,1)} async-done(((bf16[1,1024,512]{2,1,0:T(8,128)(2,1)}), bf16[4,1024,512]{2,1,0:T(8,128)(2,1)}) %all-gather.5.cloned.1.call-update) | async-done | bytes 4194320 | tf_op jit(solution)/shard_map/all_gather | solution.py:152
  99.4 4.5 convert_bitcast_fusion
  109.8 42.4 %while.22 = (s32[]{:T(128)}, bf16[4,1024,128]{1,2,0:T(8,128)(2,1)S(1)}, f32[4,2,1024,1]{2,1,3,0:T(2,128)S(1)}, bf16[4,1024,128]{1,2,0:T(8,128)(2,1)S(1)}, s32[4,...) while((s32[]{:T(128)}, ...), condition=%wide.region_5.6_spmd, body=%wide.region_2.5_spmd.sunk | while | flops 566361088 | bytes 32585864 | solution.py:156
  152.2 4.5 fusion.69
  156.9 143.1 %reduce-scatter.5.cloned.1.call-done = f32[1,1024,512]{2,1,0:T(8,128)} async-done(((f32[4,1024,512]{2,1,0:T(8,128)}), f32[1,1024,512]{2,1,0:T(8,128)}) %reduce-scatter.5.cloned.1.call-update) | async-done | bytes 2097168 | tf_op jit(solution)/shard_map/reduce_scatter | solution.py:160
  305.2 10.2 all_gather.29
  315.4 9.8 all_gather.28
  325.2 60.2 %all-gather.7.cloned.1.call-done = bf16[4,1024,512]{2,1,0:T(8,128)(2,1)} async-done(((bf16[1,1024,512]{2,1,0:T(8,128)(2,1)}), bf16[4,1024,512]{2,1,0:T(8,128)(2,1)}) %all-gather.7.cloned.1.call-update) | async-done | bytes 4194320 | tf_op jit(solution)/shard_map/all_gather | solution.py:168
  385.5 8.0 fusion.64
  393.4 72.8 %all-gather.9.cloned.1.call-done = bf16[4,1024,512]{2,1,0:T(8,128)(2,1)} async-done(((bf16[1,1024,512]{2,1,0:T(8,128)(2,1)}), bf16[4,1024,512]{2,1,0:T(8,128)(2,1)}) %all-gather.9.cloned.1.call-update) | async-done | bytes 4194320 | tf_op jit(solution)/shard_map/all_gather | solution.py:185
  466.2 10.3 convert_reduce_fusion
  478.5 4.5 convolution_convert_fusion
  483.1 8.8 convolution_convert_fusion.1
  491.9 66.5 %reduce-scatter.9.cloned.1.call-done = bf16[1,1024,512]{2,1,0:T(8,128)(2,1)} async-done(((bf16[4,1024,512]{2,1,0:T(8,128)(2,1)}), bf16[1,1024,512]{2,1,0:T(8,128)(2,1)}) %reduce-scatter.9.cloned.1.call-update) | async-done | bytes 1048592 | tf_op jit(solution)/shard_map/reduce_scatter | solution.py:197
  561.2 76.8 %reduce-scatter.7.cloned.1.call-done = bf16[1,1024,512]{2,1,0:T(8,128)(2,1)} async-done(((bf16[4,1024,512]{2,1,0:T(8,128)(2,1)}), bf16[1,1024,512]{2,1,0:T(8,128)(2,1)}) %reduce-scatter.7.cloned.1.call-update) | async-done | bytes 1048592 | tf_op jit(solution)/shard_map/reduce_scatter | solution.py:175
  644.2 81.2 %all-gather.11.cloned.1.call-done = bf16[4,1024,512]{2,1,0:T(8,128)(2,1)} async-done(((bf16[1,1024,512]{2,1,0:T(8,128)(2,1)}), bf16[4,1024,512]{2,1,0:T(8,128)(2,1)}) %all-gather.11.cloned.1.call-update) | async-done | bytes 4194320 | tf_op jit(solution)/shard_map/all_gather | solution.py:209
  725.3 3.4 convolution_convert_fusion.2
  728.8 72.6 %while.23 = (s32[]{:T(128)}, bf16[4,3,1024,128]{2,3,1,0:T(8,128)(2,1)}, bf16[4,1024,128]{1,2,0:T(8,128)(2,1)}, s32[4,1024]{1,0:T(4,128)S(1)}, s32[4]{0:T(128)S(1...) while((s32[]{:T(128)}, ...), condition=%wide.region_15.16_spmd, body=%wide.region_13.15_spmd.sunk | while | flops 1380842496 | bytes 73996440 | solution.py:214
  737.6 3.4 multiply_reduce_fusion.4
  801.4 6.3 bitcast_convert_fusion
  809.3 6.5 fusion.47
  815.9 7.1 fusion.55
  825.3 5.1 fusion.57
  831.4 3.8 all-to-all-start
  835.2 47.9 %reduce-scatter.11.cloned.1.call-done = bf16[1,1024,512]{2,1,0:T(8,128)(2,1)} async-done(((bf16[4,1024,512]{2,1,0:T(8,128)(2,1)}), bf16[1,1024,512]{2,1,0:T(8,128)(2,1)}) %reduce-scatter.11.cloned.1.call-update) | async-done | bytes 1048592 | tf_op jit(solution)/shard_map/reduce_scatter | solution.py:222
  889.0 4.2 all-to-all-start.1
  893.3 4.4 fusion.77
  900.1 10.1 all-to-all-done.1
  913.0 41.1 %all-reduce = (f32[512]{0:T(512)}, f32[512]{0:T(512)}, f32[512]{0:T(512)}, f32[512]{0:T(512)}, f32[512]{0:T(512)}, /*index=5*/f32[2048]{0:T(1024)}, f32[512]{0:T(512)}) all-reduce(f32[512]{0:T(512)} %copy-done.32, f32[512]{0:T(512)S(1)} %copy-done.38, f32[512]{0:T(512)S(1)} %copy-done.37, ...), channel_id=1, replica_groups=mesh['dp'=8,'tensor'=4] {'dp','tensor'}, use_global_device_ids=true, to_apply=%region_23.24 | all-reduce | flops 5120 | bytes 40960 | tf_op jit(solution)/shard_map/psum | solution.py:252
  954.1 77.5 %all-reduce.3.cloned.1.call-done = f32[512,512]{1,0:T(8,128)} async-done(((f32[512,512]{1,0:T(8,128)}), f32[512,512]{1,0:T(8,128)}) %all-reduce.3.cloned.1.call-update) | async-done | bytes 1048592 | tf_op jit(solution)/shard_map/psum | solution.py:252
  (270 shorter events, 159.0 us)
Async XLA Ops:
  7.2 92.1 %all-gather.5.cloned.1.call-start = ((), (), s32[]{:S(2)}) async-start(), calls=%async_computation.6 | async-start | bytes 5242880 | tf_op jit(solution)/shard_map/all_gather | solution.py:152
  9.7 290.2 %copy-start.18 = (f32[512]{0:T(512)}, f32[512]{0:T(512)S(1)}, u32[]{:S(2)}) copy-start(f32[512]{0:T(512)S(1)} %add.138) | copy-start | bytes 6148
  15.7 284.2 %reduce-scatter.5.cloned.1.call-start = ((), (), s32[]{:S(2)}) async-start(), calls=%async_computation.7 | async-start | bytes 10485760 | tf_op jit(solution)/shard_map/reduce_scatter | solution.py:160
  36.3 67.6 %copy-start.12 = (bf16[3,512,128]{2,1,0:T(8,128)(2,1)}, bf16[3,512,128]{2,1,0:T(8,128)(2,1)S(1)}, u32[]{:S(2)}) copy-start(bf16[3,512,128]{2,1,0:T(8,128)(2,1)S(1)} %all_gather.25) | copy-start | bytes 1179652
  156.8 143.2 %copy-start.2 = (bf16[1,1024,512]{2,1,0:T(8,128)(2,1)S(1)}, bf16[1,1024,512]{2,1,0:T(8,128)(2,1)}, u32[]{:S(2)}) copy-start(bf16[1,1024,512]{2,1,0:T(8,128)(2,1)} %param.21) | copy-start | bytes 3145732
  156.8 145.5 %copy-start.31 = (f32[512]{0:T(512)S(1)}, f32[512]{0:T(512)}, u32[]{:S(2)}) copy-start(f32[512]{0:T(512)} %param.33) | copy-start | bytes 6148
  156.8 145.5 %copy-start.43 = (f32[512]{0:T(512)S(1)}, f32[512]{0:T(512)}, u32[]{:S(2)}) copy-start(f32[512]{0:T(512)} %param.34) | copy-start | bytes 6148
  156.8 228.6 %all-gather.7.cloned.1.call-start = ((), (), s32[]{:S(2)}) async-start(), calls=%async_computation.8 | async-start | bytes 5242880 | tf_op jit(solution)/shard_map/all_gather | solution.py:168
  303.7 162.5 %all-gather.9.cloned.1.call-start = ((), (), s32[]{:S(2)}) async-start(), calls=%async_computation.10 | async-start | bytes 5242880 | tf_op jit(solution)/shard_map/all_gather | solution.py:185
  304.3 254.1 %reduce-scatter.9.cloned.1.call-start = ((), (), s32[]{:S(2)}) async-start(), calls=%async_computation.11 | async-start | bytes 5242880 | tf_op jit(solution)/shard_map/reduce_scatter | solution.py:197
  483.0 155.0 %reduce-scatter.7.cloned.1.call-start = ((), (), s32[]{:S(2)}) async-start(), calls=%async_computation.9 | async-start | bytes 5242880 | tf_op jit(solution)/shard_map/reduce_scatter | solution.py:175
  491.8 146.2 %copy-start.44 = (f32[512]{0:T(512)S(1)}, f32[512]{0:T(512)}, u32[]{:S(2)}) copy-start(f32[512]{0:T(512)} %param.36) | copy-start | bytes 6148
  491.9 233.5 %all-gather.11.cloned.1.call-start = ((), (), s32[]{:S(2)}) async-start(), calls=%async_computation.12 | async-start | bytes 5242880 | tf_op jit(solution)/shard_map/all_gather | solution.py:209
  561.2 81.3 %copy-start.8 = (bf16[1,1024,512]{2,1,0:T(8,128)(2,1)S(1)}, bf16[1,1024,512]{2,1,0:T(8,128)(2,1)}, u32[]{:S(2)}) copy-start(bf16[1,1024,512]{2,1,0:T(8,128)(2,1)} %param.37) | copy-start | bytes 3145732
  641.2 87.6 %copy-start.24 = (f32[1024]{0:T(1024)}, f32[1024]{0:T(1024)S(1)}, u32[]{:S(2)}) copy-start(f32[1024]{0:T(1024)S(1)} %negate_multiply_fusion.1) | copy-start | bytes 12292
  643.9 239.2 %reduce-scatter.11.cloned.1.call-start = ((), (), s32[]{:S(2)}) async-start(), calls=%async_computation.13 | async-start | bytes 5242880 | tf_op jit(solution)/shard_map/reduce_scatter | solution.py:222
  728.8 72.6 %copy-start.13 = (bf16[3,512,128]{2,1,0:T(8,128)(2,1)S(1)}, bf16[3,512,128]{2,1,0:T(8,128)(2,1)}, u32[]{:S(2)}) copy-start(bf16[3,512,128]{2,1,0:T(8,128)(2,1)} %copy-done.12) | copy-start | bytes 1179652
  825.3 57.9 %copy-start.3 = (bf16[1,1024,512]{2,1,0:T(8,128)(2,1)S(1)}, bf16[1,1024,512]{2,1,0:T(8,128)(2,1)}, u32[]{:S(2)}) copy-start(bf16[1,1024,512]{2,1,0:T(8,128)(2,1)} %param.21) | copy-start | bytes 3145732
  825.3 57.9 %copy-start.15 = (f32[1024]{0:T(1024)S(1)}, f32[1024]{0:T(1024)}, u32[]{:S(2)}) copy-start(f32[1024]{0:T(1024)} %copy-done.14) | copy-start | bytes 12292
  825.3 57.9 %copy-start.19 = (f32[512]{0:T(512)S(1)}, f32[512]{0:T(512)}, u32[]{:S(2)}) copy-start(f32[512]{0:T(512)} %copy-done.18) | copy-start | bytes 6148
  825.3 57.9 %copy-start.30 = (f32[512]{0:T(512)S(1)}, f32[512]{0:T(512)}, u32[]{:S(2)}) copy-start(f32[512]{0:T(512)} %param.31) | copy-start | bytes 6148
  830.4 55.4 %copy-start.26 = (f32[1024]{0:T(1024)S(1)}, f32[1024]{0:T(1024)}, u32[]{:S(2)}) copy-start(f32[1024]{0:T(1024)} %copy-done.25) | copy-start | bytes 12292
  830.4 55.4 %copy-start.23 = (f32[1024]{0:T(1024)S(1)}, f32[1024]{0:T(1024)}, u32[]{:S(2)}) copy-start(f32[1024]{0:T(1024)} %copy-done.22) | copy-start | bytes 12292
  830.7 62.7 %copy-start.9 = (bf16[1,1024,512]{2,1,0:T(8,128)(2,1)S(1)}, bf16[1,1024,512]{2,1,0:T(8,128)(2,1)}, u32[]{:S(2)}) copy-start(bf16[1,1024,512]{2,1,0:T(8,128)(2,1)} %param.37) | copy-start | bytes 3145732
  831.4 57.5 %all-to-all-start = ((bf16[8,3,64,128]{3,2,1,0:T(8,128)(2,1)}), bf16[8,3,64,128]{3,2,1,0:T(8,128)(2,1)S(1)}, u32[]{:S(2)}, u32[]{:S(2)}) async-start(bf16[8,3,64,128]{3,2,1,0:T(8,128)(2,1)} %copy.79), calls=%async_computation.4 | async-start | bytes 786432 | tf_op jit(solution)/shard_map/all_to_all | solution.py:21
  889.0 21.2 %all-to-all-start.1 = ((bf16[8,64,1152]{2,1,0:T(8,128)(2,1)}), bf16[8,64,1152]{2,1,0:T(8,128)(2,1)}, u32[]{:S(2)}, u32[]{:S(2)}) async-start(bf16[8,64,1152]{2,1,0:T(8,128)(2,1)} %bitcast.206), calls=%async_computation.5 | async-start | bytes 2359296 | tf_op jit(solution)/shard_map/all_to_all | solution.py:21
  893.2 138.4 %all-reduce.3.cloned.1.call-start = ((), (), s32[]{:S(2)}) async-start(), calls=%async_computation.14 | async-start | bytes 2097152 | tf_op jit(solution)/shard_map/psum | solution.py:252
  893.3 140.6 %copy-start.1 = (f32[512,512]{1,0:T(8,128)S(1)}, f32[512,512]{1,0:T(8,128)}, u32[]{:S(2)}) copy-start(f32[512,512]{1,0:T(8,128)} %param.29) | copy-start | bytes 3145732
  897.7 15.3 %copy-start.38 = (f32[512]{0:T(512)S(1)}, f32[512]{0:T(512)}, u32[]{:S(2)}) copy-start(f32[512]{0:T(512)} %get-tuple-element.160) | copy-start | bytes 6148
  897.7 15.3 %copy-start.40 = (f32[512]{0:T(512)S(1)}, f32[512]{0:T(512)}, u32[]{:S(2)}) copy-start(f32[512]{0:T(512)} %get-tuple-element.158) | copy-start | bytes 6148
  897.7 15.3 %copy-start.41 = (f32[512]{0:T(512)S(1)}, f32[512]{0:T(512)}, u32[]{:S(2)}) copy-start(f32[512]{0:T(512)} %get-tuple-element.162) | copy-start | bytes 6148
  897.7 15.3 %copy-start.42 = (f32[512]{0:T(512)S(1)}, f32[512]{0:T(512)}, u32[]{:S(2)}) copy-start(f32[512]{0:T(512)} %get-tuple-element.224) | copy-start | bytes 6148
  (27 other events, 133.7 us)
Sparse Core Ops, SparseCore 0:
  15.9 83.4 all-gather.4
  156.9 142.9 reduce-scatter.4
  303.9 81.5 all-gather.6
  386.9 79.2 all-gather.8
  483.1 75.2 reduce-scatter.8
  560.7 77.2 reduce-scatter.6
  644.0 81.2 all-gather.10
  807.8 75.2 reduce-scatter.10
  900.7 130.9 all-reduce.2
where the time goes:
time: 1040 us
  waiting for transfers between devices  700 us (67%)
  matrix products  127 us (12%)
  blocking collectives  81.5 us (8%)
  other arithmetic  71.6 us (7%)
  local copies, waits for them, and re-layouts  35.8 us (3%)
  between operations  15.5 us (1%)
    reduce_scatter x1, waiting for transfers between devices, shards(): lax.psum_scatter(jnp.einsum('nse,de->nsd', part_rows, out_copy, preferred...  143 us
    all_gather x1, waiting for transfers between devices, shards(): grad_attn_all = lax.all_gather(grad_attn, 'tensor', axis=0, tiled=True)  81.2 us
    psum x1, waiting for transfers between devices, shards(): lax.psum((grad_time_w, grad_time_bias, grad_gain_one, grad_bias_one, grad...  77.5 us
    reduce_scatter x1, waiting for transfers between devices, shards(): lax.psum_scatter(jnp.einsum('nsf,df->nsd', part_rows, down_copy, preferre...  76.8 us
    all_gather x1, waiting for transfers between devices, shards(): grad_out_all = lax.all_gather(cotangent, 'tensor', axis=0, tiled=True)  72.8 us
    reduce_scatter x1, waiting for transfers between devices, shards(): lax.psum_scatter(jnp.einsum('nsf,df->nsd', part_rows, up_copy, preferred_...  66.5 us
    all_gather x1, waiting for transfers between devices, shards(): normed_all = lax.all_gather(normed_one, 'tensor', axis=0, tiled=True)  63.1 us
    all_gather x1, waiting for transfers between devices, shards(): second_all = lax.all_gather(normed_two, 'tensor', axis=0, tiled=True)  60.2 us
  transfers between devices with their start and end apart: 11, of which 10 were waited for; matrix products, arithmetic and copies ran while one was open for 6% of the time, Pallas kernels for 0%

commit v1 on v0

--- a/solution.py
+++ b/solution.py
@@ -182,7 +182,17 @@
     ).astype(jnp.float32)
     layer_out = (middle + ffn_out + b_down).astype(jnp.bfloat16)
     grad_b_down = jnp.sum(cotangent.astype(jnp.float32), axis=(0, 1))
-    grad_out_all = lax.all_gather(cotangent, "tensor", axis=0, tiled=True)
+    shard = cotangent
+    ways, here, step = (lax.axis_size("tensor"), lax.axis_index("tensor"), shard.shape[0])
+    dims = [n * ways if d == 0 else n for d, n in enumerate(shard.shape)]
+    grad_out_all = lax.dynamic_update_slice_in_dim(
+        jnp.zeros(dims, shard.dtype), shard, here * step, axis=0
+    )
+    for far in range(1, ways):
+        shard = lax.ppermute(shard, "tensor", [(d, (d + 1) % ways) for d in range(ways)])
+        grad_out_all = lax.dynamic_update_slice_in_dim(
+            grad_out_all, shard, (here - far) % ways * step, axis=0
+        )
     grad_down = jnp.einsum(
         "nsd,nsf->df", grad_out_all, activated, preferred_element_type=jnp.float32
     )

time: 1040 us -> 1040 us (level)
  waiting for transfers between devices: 700 us -> 650 us
  starting transfers between devices: 8.57 us -> 40.4 us
    ppermute x0 -> x3, waiting for transfers between devices: none -> 83 us  [shards(): lax.ppermute(shard, 'tensor', [(d, (d + 1) % ways) for d in range(ways)])]
    all_gather x1 -> x0, waiting for transfers between devices: 72.8 us -> none  [shards(): grad_out_all = lax.all_gather(cotangent, 'tensor', axis=0, tiled=True)]
    all_gather x1, waiting for transfers between devices: 60.2 us -> 0.01 us  [shards(): second_all = lax.all_gather(normed_two, 'tensor', axis=0, tiled=True)]
    ppermute x0 -> x3, starting transfers between devices: none -> 32.1 us  [shards(): lax.ppermute(shard, 'tensor', [(d, (d + 1) % ways) for d in range(ways)])]
  transfers between devices with their start and end apart: 11 -> 13, of which waited for: 10 -> 10; matrix products, arithmetic and copies ran while one was open for 6% -> 6% of each run, Pallas kernels for 0% -> 0%
where the time goes in v1:
time: 1040 us; the launch traced here: 1030 us
  waiting for transfers between devices  650 us (62%)
  matrix products  126 us (12%)
  blocking collectives  83.5 us (8%)
  other arithmetic  72.5 us (7%)
  local copies, waits for them, and re-layouts  45.8 us (4%)
  starting transfers between devices  40.4 us (4%)
  between operations  15.8 us (2%)
    reduce_scatter x1, waiting for transfers between devices, shards(): lax.psum_scatter(jnp.einsum('nse,de->nsd', part_rows, out_copy, preferred...  143 us
    ppermute x3, waiting for transfers between devices, shards(): lax.ppermute(shard, 'tensor', [(d, (d + 1) % ways) for d in range(ways)])  83 us
    all_gather x1, waiting for transfers between devices, shards(): grad_attn_all = lax.all_gather(grad_attn, 'tensor', axis=0, tiled=True)  81.2 us
    psum x1, waiting for transfers between devices, shards(): lax.psum((grad_time_w, grad_time_bias, grad_gain_one, grad_bias_one, grad...  77.5 us
    reduce_scatter x1, waiting for transfers between devices, shards(): lax.psum_scatter(jnp.einsum('nsf,df->nsd', part_rows, down_copy, preferre...  76.8 us
    reduce_scatter x1, waiting for transfers between devices, shards(): lax.psum_scatter(jnp.einsum('nsf,df->nsd', part_rows, up_copy, preferred_...  67.2 us
    all_gather x1, waiting for transfers between devices, shards(): normed_all = lax.all_gather(normed_one, 'tensor', axis=0, tiled=True)  63.1 us
    reduce_scatter x1, waiting for transfers between devices, shards(): lax.psum_scatter(jnp.einsum('ncse,cde->nsd', part_rows, qkv_copy, preferr...  47.6 us
  transfers between devices with their start and end apart: 13, of which 10 were waited for; matrix products, arithmetic and copies ran while one was open for 6% of the time, Pallas kernels for 0%

profile of v1, /device:TPU:0, one launch (start us, length us, event | category | flops | bytes accessed | tf_op | source)
XLA Modules:
  0.0 1033.9 jit_solution(12299230444967236747)
XLA Ops:
  15.9 10.7 %all_gather.23 = bf16[512,128]{1,0:T(8,128)(2,1)S(1)} all-gather(bf16[64,128]{1,0:T(8,128)(2,1)S(1)} %convert_element_type.130), channel_id=1, replica_groups=mesh['dp'=8,'tensor'=4] {'dp'}, dimensions={0}, use_global_device_ids=true | all-gather | bytes 147456 | tf_op jit(solution)/shard_map/all_gather | solution.py:140
  26.6 9.7 all_gather.22
  36.3 63.1 %all-gather.4.cloned.1.call-done = bf16[4,1024,512]{2,1,0:T(8,128)(2,1)} async-done(((bf16[1,1024,512]{2,1,0:T(8,128)(2,1)}), bf16[4,1024,512]{2,1,0:T(8,128)(2,1)}) %all-gather.4.cloned.1.call-update) | async-done | bytes 4194320 | tf_op jit(solution)/shard_map/all_gather | solution.py:152
  99.4 4.5 convert_bitcast_fusion
  109.8 42.4 %while.22 = (s32[]{:T(128)}, bf16[4,1024,128]{1,2,0:T(8,128)(2,1)S(1)}, f32[4,2,1024,1]{2,1,3,0:T(2,128)S(1)}, bf16[4,1024,128]{1,2,0:T(8,128)(2,1)S(1)}, s32[4,...) while((s32[]{:T(128)}, ...), condition=%wide.region_5.6_spmd, body=%wide.region_2.5_spmd.sunk | while | flops 566361088 | bytes 32585864 | solution.py:156
  152.2 4.5 fusion.68
  156.9 143.1 %reduce-scatter.5.cloned.1.call-done = f32[1,1024,512]{2,1,0:T(8,128)} async-done(((f32[4,1024,512]{2,1,0:T(8,128)}), f32[1,1024,512]{2,1,0:T(8,128)}) %reduce-scatter.5.cloned.1.call-update) | async-done | bytes 2097168 | tf_op jit(solution)/shard_map/reduce_scatter | solution.py:160
  305.1 39.6 %collective-permute-done = bf16[1,1024,512]{2,1,0:T(8,128)(2,1)S(1)} collective-permute-done((bf16[1,1024,512]{2,1,0:T(8,128)(2,1)S(1)}, bf16[1,1024,512]{2,1,0:T(8,128)(2,1)S(1)}, u32[]{:S(2)}, u32[]{:S(2)}) %collective-permute-start) | collective-permute-done | bytes 1048608 | tf_op jit(solution)/shard_map/ppermute | solution.py:192
  345.6 18.6 %collective-permute-start.1 = (bf16[1,1024,512]{2,1,0:T(8,128)(2,1)S(1)}, bf16[1,1024,512]{2,1,0:T(8,128)(2,1)}, u32[]{:S(2)}, u32[]{:S(2)}) collective-permute-start(bf16[1,1024,512]{2,1,0:T(8,128)(2,1)S(1)} %collective-permute-done), channel_id=1, source_target_pairs={{0,1},{1,2},{2,3},{3,0},{4,5},{5,6},{6,7},{7,4},{8,9},{9,10},{10,1... | collective-permute-start | bytes 3145736 | tf_op jit(solution)/shard_map/ppermute | solution.py:192
  364.2 43.4 %collective-permute-done.1 = bf16[1,1024,512]{2,1,0:T(8,128)(2,1)} collective-permute-done((bf16[1,1024,512]{2,1,0:T(8,128)(2,1)S(1)}, bf16[1,1024,512]{2,1,0:T(8,128)(2,1)}, u32[]{:S(2)}, u32[]{:S(2)}) %collective-permute-start.1) | collective-permute-done | bytes 1048608 | tf_op jit(solution)/shard_map/ppermute | solution.py:192
  407.6 12.3 %collective-permute-start.2 = (bf16[1,1024,512]{2,1,0:T(8,128)(2,1)}, bf16[1,1024,512]{2,1,0:T(8,128)(2,1)}, u32[]{:S(2)}, u32[]{:S(2)}) collective-permute-start(bf16[1,1024,512]{2,1,0:T(8,128)(2,1)} %collective-permute-done.1), channel_id=1, source_target_pairs={{0,1},{1,2},{2,3},{3,0},{4,5},{5,6},{6,7},{7,4},{8,9},{9,10},{10,1... | collective-permute-start | bytes 3145736 | tf_op jit(solution)/shard_map/ppermute | solution.py:192
  421.8 11.2 %all_gather.26 = bf16[512,512]{1,0:T(8,128)(2,1)} all-gather(bf16[64,512]{1,0:T(8,128)(2,1)S(1)} %convert_element_type.134), channel_id=1, replica_groups=mesh['dp'=8,'tensor'=4] {'dp'}, dimensions={0}, use_global_device_ids=true | all-gather | bytes 589824 | tf_op jit(solution)/shard_map/all_gather | solution.py:142
  433.0 10.7 %all_gather.25 = bf16[512,512]{1,0:T(8,128)(2,1)} all-gather(bf16[64,512]{1,0:T(8,128)(2,1)S(1)} %convert_element_type.132), channel_id=1, replica_groups=mesh['dp'=8,'tensor'=4] {'dp'}, dimensions={0}, use_global_device_ids=true | all-gather | bytes 589824 | tf_op jit(solution)/shard_map/all_gather | solution.py:141
  452.7 4.8 fusion.63
  457.5 11.0 %convert_reduce_fusion = (f32[512]{0:T(512)S(1)}, bf16[4,1024,512]{2,1,0:T(8,128)(2,1)S(1)}) fusion(f32[4,1024,512]{2,1,0:T(8,128)S(1)} %fusion.63, f32[512]{0:T(512)S(1)} %dynamic_slice.43, bf16[4,1024,512]{2,1,0:T(8,128)(2,1)} %constant_dynamic-update-slice_fusion.1, bf16[512,512]{1,0:T(8,128)(2,1)S(1)} %copy-done.16), kind=kOutput, calls=%fused_computation.53 | convolution fusion | flops 2195717632 | bytes 17305600 | tf_op jit(solution)/shard_map/nsd,df->nsf/dot_general | solution.py:199
  470.5 4.6 convolution_convert_fusion
  475.2 8.9 convolution_convert_fusion.1
  484.1 67.2 %reduce-scatter.9.cloned.1.call-done = bf16[1,1024,512]{2,1,0:T(8,128)(2,1)} async-done(((bf16[4,1024,512]{2,1,0:T(8,128)(2,1)}), bf16[1,1024,512]{2,1,0:T(8,128)(2,1)}) %reduce-scatter.9.cloned.1.call-update) | async-done | bytes 1048592 | tf_op jit(solution)/shard_map/reduce_scatter | solution.py:207
  554.1 76.8 %reduce-scatter.7.cloned.1.call-done = bf16[1,1024,512]{2,1,0:T(8,128)(2,1)} async-done(((bf16[4,1024,512]{2,1,0:T(8,128)(2,1)}), bf16[1,1024,512]{2,1,0:T(8,128)(2,1)}) %reduce-scatter.7.cloned.1.call-update) | async-done | bytes 1048592 | tf_op jit(solution)/shard_map/reduce_scatter | solution.py:175
  637.0 81.2 %all-gather.8.cloned.1.call-done = bf16[4,1024,512]{2,1,0:T(8,128)(2,1)} async-done(((bf16[1,1024,512]{2,1,0:T(8,128)(2,1)}), bf16[4,1024,512]{2,1,0:T(8,128)(2,1)}) %all-gather.8.cloned.1.call-update) | async-done | bytes 4194320 | tf_op jit(solution)/shard_map/all_gather | solution.py:219
  721.7 72.6 %while.23 = (s32[]{:T(128)}, bf16[4,3,1024,128]{2,3,1,0:T(8,128)(2,1)}, bf16[4,1024,128]{1,2,0:T(8,128)(2,1)}, s32[4,1024]{1,0:T(4,128)S(1)}, s32[4]{0:T(128)S(1...) while((s32[]{:T(128)}, ...), condition=%wide.region_15.16_spmd, body=%wide.region_13.15_spmd.sunk | while | flops 1380842496 | bytes 73996440 | solution.py:224
  794.3 6.3 bitcast_convert_fusion
  802.2 6.2 fusion.47
  808.5 8.1 fusion.48
  818.9 5.1 fusion.56
  825.0 3.5 all-to-all-start
  828.4 47.6 %reduce-scatter.11.cloned.1.call-done = bf16[1,1024,512]{2,1,0:T(8,128)(2,1)} async-done(((bf16[4,1024,512]{2,1,0:T(8,128)(2,1)}), bf16[1,1024,512]{2,1,0:T(8,128)(2,1)}) %reduce-scatter.11.cloned.1.call-update) | async-done | bytes 1048592 | tf_op jit(solution)/shard_map/reduce_scatter | solution.py:232
  881.9 4.3 all-to-all-start.1
  886.3 4.4 fusion.76
  893.0 10.1 all-to-all-done.1
  905.9 41.1 %all-reduce = (f32[512]{0:T(512)}, f32[512]{0:T(512)}, f32[512]{0:T(512)}, f32[512]{0:T(512)}, f32[512]{0:T(512)}, /*index=5*/f32[2048]{0:T(1024)}, f32[512]{0:T(512)}) all-reduce(f32[512]{0:T(512)} %copy-done.36, f32[512]{0:T(512)S(1)} %copy-done.42, f32[512]{0:T(512)S(1)} %copy-done.41, ...), channel_id=1, replica_groups=mesh['dp'=8,'tensor'=4] {'dp','tensor'}, use_global_device_ids=true, to_apply=%region_23.24 | all-reduce | flops 5120 | bytes 40960 | tf_op jit(solution)/shard_map/psum | solution.py:262
  947.0 77.5 %all-reduce.3.cloned.1.call-done = f32[512,512]{1,0:T(8,128)} async-done(((f32[512,512]{1,0:T(8,128)}), f32[512,512]{1,0:T(8,128)}) %all-reduce.3.cloned.1.call-update) | async-done | bytes 1048592 | tf_op jit(solution)/shard_map/psum | solution.py:262
  (284 shorter events, 177.4 us)
Async XLA Ops:
  7.2 92.1 %all-gather.4.cloned.1.call-start = ((), (), s32[]{:S(2)}) async-start(), calls=%async_computation.6 | async-start | bytes 5242880 | tf_op jit(solution)/shard_map/all_gather | solution.py:152
  9.7 290.2 %copy-start.22 = (f32[512]{0:T(512)}, f32[512]{0:T(512)S(1)}, u32[]{:S(2)}) copy-start(f32[512]{0:T(512)S(1)} %add.163) | copy-start | bytes 6148
  15.7 284.2 %reduce-scatter.5.cloned.1.call-start = ((), (), s32[]{:S(2)}) async-start(), calls=%async_computation.7 | async-start | bytes 10485760 | tf_op jit(solution)/shard_map/reduce_scatter | solution.py:160
  36.3 67.6 %copy-start.17 = (bf16[3,512,128]{2,1,0:T(8,128)(2,1)}, bf16[3,512,128]{2,1,0:T(8,128)(2,1)S(1)}, u32[]{:S(2)}) copy-start(bf16[3,512,128]{2,1,0:T(8,128)(2,1)S(1)} %all_gather.22) | copy-start | bytes 1179652
  156.8 143.2 %copy-start.2 = (bf16[1,1024,512]{2,1,0:T(8,128)(2,1)S(1)}, bf16[1,1024,512]{2,1,0:T(8,128)(2,1)}, u32[]{:S(2)}) copy-start(bf16[1,1024,512]{2,1,0:T(8,128)(2,1)} %param.21) | copy-start | bytes 3145732
  156.8 145.5 %copy-start.35 = (f32[512]{0:T(512)S(1)}, f32[512]{0:T(512)}, u32[]{:S(2)}) copy-start(f32[512]{0:T(512)} %param.33) | copy-start | bytes 6148
  156.8 145.5 %copy-start.47 = (f32[512]{0:T(512)S(1)}, f32[512]{0:T(512)}, u32[]{:S(2)}) copy-start(f32[512]{0:T(512)} %param.34) | copy-start | bytes 6148
  156.8 295.9 %all-gather.6.cloned.1.call-start = ((), (), s32[]{:S(2)}) async-start(), calls=%async_computation.8 | async-start | bytes 5242880 | tf_op jit(solution)/shard_map/all_gather | solution.py:168
  301.9 118.0 %copy-start.21 = (f32[64,512]{1,0:T(8,128)S(1)}, f32[64,512]{1,0:T(8,128)}, u32[]{:S(2)}) copy-start(f32[64,512]{1,0:T(8,128)} %param.27) | copy-start | bytes 393220
  303.8 247.6 %reduce-scatter.9.cloned.1.call-start = ((), (), s32[]{:S(2)}) async-start(), calls=%async_computation.10 | async-start | bytes 5242880 | tf_op jit(solution)/shard_map/reduce_scatter | solution.py:207
  303.8 40.8 %collective-permute-start = (bf16[1,1024,512]{2,1,0:T(8,128)(2,1)S(1)}, bf16[1,1024,512]{2,1,0:T(8,128)(2,1)S(1)}, u32[]{:S(2)}, u32[]{:S(2)}) collective-permute-start(bf16[1,1024,512]{2,1,0:T(8,128)(2,1)S(1)} %copy-done.8), channel_id=1, source_target_pairs={{0,1},{1,2},{2,3},{3,0},{4,5},{5,6},{6,7},{7,4},{8,9},{9,10},{10,1... | collective-permute-start | bytes 3145736 | tf_op jit(solution)/shard_map/ppermute | solution.py:192
  345.6 62.0 %collective-permute-start.1 = (bf16[1,1024,512]{2,1,0:T(8,128)(2,1)S(1)}, bf16[1,1024,512]{2,1,0:T(8,128)(2,1)}, u32[]{:S(2)}, u32[]{:S(2)}) collective-permute-start(bf16[1,1024,512]{2,1,0:T(8,128)(2,1)S(1)} %collective-permute-done), channel_id=1, source_target_pairs={{0,1},{1,2},{2,3},{3,0},{4,5},{5,6},{6,7},{7,4},{8,9},{9,10},{10,1... | collective-permute-start | bytes 3145736 | tf_op jit(solution)/shard_map/ppermute | solution.py:192
  407.6 42.8 %collective-permute-start.2 = (bf16[1,1024,512]{2,1,0:T(8,128)(2,1)}, bf16[1,1024,512]{2,1,0:T(8,128)(2,1)}, u32[]{:S(2)}, u32[]{:S(2)}) collective-permute-start(bf16[1,1024,512]{2,1,0:T(8,128)(2,1)} %collective-permute-done.1), channel_id=1, source_target_pairs={{0,1},{1,2},{2,3},{3,0},{4,5},{5,6},{6,7},{7,4},{8,9},{9,10},{10,1... | collective-permute-start | bytes 3145736 | tf_op jit(solution)/shard_map/ppermute | solution.py:192
  420.9 26.2 %copy-start.15 = (bf16[1,1024,512]{2,1,0:T(8,128)(2,1)S(1)}, bf16[1,1024,512]{2,1,0:T(8,128)(2,1)}, u32[]{:S(2)}) copy-start(bf16[1,1024,512]{2,1,0:T(8,128)(2,1)} %copy-done.14) | copy-start | bytes 3145732
  475.1 155.8 %reduce-scatter.7.cloned.1.call-start = ((), (), s32[]{:S(2)}) async-start(), calls=%async_computation.9 | async-start | bytes 5242880 | tf_op jit(solution)/shard_map/reduce_scatter | solution.py:175
  484.0 146.9 %copy-start.48 = (f32[512]{0:T(512)S(1)}, f32[512]{0:T(512)}, u32[]{:S(2)}) copy-start(f32[512]{0:T(512)} %param.36) | copy-start | bytes 6148
  484.1 234.2 %all-gather.8.cloned.1.call-start = ((), (), s32[]{:S(2)}) async-start(), calls=%async_computation.11 | async-start | bytes 5242880 | tf_op jit(solution)/shard_map/all_gather | solution.py:219
  634.1 87.6 %copy-start.28 = (f32[1024]{0:T(1024)}, f32[1024]{0:T(1024)S(1)}, u32[]{:S(2)}) copy-start(f32[1024]{0:T(1024)S(1)} %negate_multiply_fusion.1) | copy-start | bytes 12292
  636.8 239.3 %reduce-scatter.11.cloned.1.call-start = ((), (), s32[]{:S(2)}) async-start(), calls=%async_computation.12 | async-start | bytes 5242880 | tf_op jit(solution)/shard_map/reduce_scatter | solution.py:232
  721.7 72.6 %copy-start.18 = (bf16[3,512,128]{2,1,0:T(8,128)(2,1)S(1)}, bf16[3,512,128]{2,1,0:T(8,128)(2,1)}, u32[]{:S(2)}) copy-start(bf16[3,512,128]{2,1,0:T(8,128)(2,1)} %copy-done.17) | copy-start | bytes 1179652
  818.8 57.2 %copy-start.3 = (bf16[1,1024,512]{2,1,0:T(8,128)(2,1)S(1)}, bf16[1,1024,512]{2,1,0:T(8,128)(2,1)}, u32[]{:S(2)}) copy-start(bf16[1,1024,512]{2,1,0:T(8,128)(2,1)} %param.21) | copy-start | bytes 3145732
  818.8 57.2 %copy-start.20 = (f32[1024]{0:T(1024)S(1)}, f32[1024]{0:T(1024)}, u32[]{:S(2)}) copy-start(f32[1024]{0:T(1024)} %copy-done.19) | copy-start | bytes 12292
  818.8 57.2 %copy-start.23 = (f32[512]{0:T(512)S(1)}, f32[512]{0:T(512)}, u32[]{:S(2)}) copy-start(f32[512]{0:T(512)} %copy-done.22) | copy-start | bytes 6148
  818.8 57.2 %copy-start.34 = (f32[512]{0:T(512)S(1)}, f32[512]{0:T(512)}, u32[]{:S(2)}) copy-start(f32[512]{0:T(512)} %param.31) | copy-start | bytes 6148
  824.0 54.8 %copy-start.30 = (f32[1024]{0:T(1024)S(1)}, f32[1024]{0:T(1024)}, u32[]{:S(2)}) copy-start(f32[1024]{0:T(1024)} %copy-done.29) | copy-start | bytes 12292
  824.0 54.8 %copy-start.27 = (f32[1024]{0:T(1024)S(1)}, f32[1024]{0:T(1024)}, u32[]{:S(2)}) copy-start(f32[1024]{0:T(1024)} %copy-done.26) | copy-start | bytes 12292
  824.2 62.0 %copy-start.9 = (bf16[1,1024,512]{2,1,0:T(8,128)(2,1)S(1)}, bf16[1,1024,512]{2,1,0:T(8,128)(2,1)}, u32[]{:S(2)}) copy-start(bf16[1,1024,512]{2,1,0:T(8,128)(2,1)} %param.37) | copy-start | bytes 3145732
  825.0 56.9 %all-to-all-start = ((bf16[8,3,64,128]{3,2,1,0:T(8,128)(2,1)}), bf16[8,3,64,128]{3,2,1,0:T(8,128)(2,1)S(1)}, u32[]{:S(2)}, u32[]{:S(2)}) async-start(bf16[8,3,64,128]{3,2,1,0:T(8,128)(2,1)} %copy.79), calls=%async_computation.4 | async-start | bytes 786432 | tf_op jit(solution)/shard_map/all_to_all | solution.py:21
  881.9 21.2 %all-to-all-start.1 = ((bf16[8,64,1152]{2,1,0:T(8,128)(2,1)}), bf16[8,64,1152]{2,1,0:T(8,128)(2,1)}, u32[]{:S(2)}, u32[]{:S(2)}) async-start(bf16[8,64,1152]{2,1,0:T(8,128)(2,1)} %bitcast.202), calls=%async_computation.5 | async-start | bytes 2359296 | tf_op jit(solution)/shard_map/all_to_all | solution.py:21
  886.2 138.4 %all-reduce.3.cloned.1.call-start = ((), (), s32[]{:S(2)}) async-start(), calls=%async_computation.13 | async-start | bytes 2097152 | tf_op jit(solution)/shard_map/psum | solution.py:262
  886.3 140.6 %copy-start.1 = (f32[512,512]{1,0:T(8,128)S(1)}, f32[512,512]{1,0:T(8,128)}, u32[]{:S(2)}) copy-start(f32[512,512]{1,0:T(8,128)} %param.29) | copy-start | bytes 3145732
  890.6 15.3 %copy-start.45 = (f32[512]{0:T(512)S(1)}, f32[512]{0:T(512)}, u32[]{:S(2)}) copy-start(f32[512]{0:T(512)} %get-tuple-element.162) | copy-start | bytes 6148
  (32 other events, 201.8 us)
Sparse Core Ops, SparseCore 0:
  15.9 83.4 all-gather.3
  156.9 142.9 reduce-scatter.4
  303.9 116.8 all-gather.5
  475.2 76.0 reduce-scatter.8
  553.6 77.2 reduce-scatter.6
  636.9 81.2 all-gather.7
  800.8 75.2 reduce-scatter.10
  893.6 130.9 all-reduce.2
